TPU v7x, 256 devices: a whole 4x4x8 slice. The times are simulated.
256 devices in a mesh: upd: 8 (over x, core), col: 32 (over z, y).
Axes of the slice: x: 4, y: 4, z: 8, core: 2. Of those that a mesh axis runs over, the one named last changes fastest.
Arguments:
- panel: bfloat16 [32, 8, 1024, 1024], P('col', None, 'upd'), may hold values from -6 to 6
- diag_tiles: bfloat16 [32, 1024, 1024], P('col', 'upd'), may hold values from -6 to 6
- dinv: bfloat16 [32, 1024, 1024], P('col'), may hold values from -1 to 1, as said below
- u_fac: bfloat16 [32, 8, 8, 96, 1024], P('col', None, 'upd'), may hold values from -1.1953125 to 1.1953125
- v_fac: bfloat16 [32, 8, 8, 96, 1024], P('col', None, 'upd'), may hold values from -1.1953125 to 1.1953125
- ranks: int32 [32, 8, 8], P('col', None, 'upd'), may hold values from 1 to 96, as said below
- sketch: bfloat16 [32, 64, 1024], P('col'), may hold values from -6 to 6
Outputs:
- panel_out: bfloat16 [32, 8, 1024, 1024], P('col', None, 'upd')
- diag_out: float32 [32, 1024, 1024], P('col', 'upd')
Inputs may be any that keep to these rules, and one draw needn't show every extreme that they name: `ranks`: in every panel tile at least two of the 8 pieces have rank 96. `dinv`: each block is lower triangular with a positive diagonal.
All inputs are finite; a program needn't handle non-finite values.
Results may differ from a plain program's by a relative error of at most 0.014.
Values may be sent and summed in bfloat16 or wider, within the bound.
No kernel may reach another device: no remote copies, remote signals or barrier semaphores. Data moves between devices by JAX's collectives and lax.ppermute only.
A program may use at most 64 MiB of HBM per device.

v0:
```python
import jax
import jax.numpy as jnp
from jax import lax
from jax.sharding import PartitionSpec as P


def in_blocks(array, dim, peers):
    dims = array.shape
    parts = array.reshape(*dims[:dim], peers, dims[dim] // peers, *dims[dim + 1 :])
    return jnp.moveaxis(parts, dim, 0)


def sum_at_owner(array, axis, dim):
    parts = in_blocks(array, dim, lax.axis_size(axis))
    arrived = lax.all_to_all(parts, axis, split_axis=0, concat_axis=0, tiled=True)
    return arrived.astype(jnp.float32).sum(axis=0)


def copy_for_each(array, axis):
    peers = lax.axis_size(axis)
    return lax.all_to_all(
        jnp.broadcast_to(array[None], (peers, *array.shape)), axis, 0, 0, tiled=True
    )


def laid_out(parts, dim):
    parts = jnp.moveaxis(parts, 0, dim)
    dims = parts.shape
    return parts.reshape(*dims[:dim], dims[dim] * dims[dim + 1], *dims[dim + 2 :])


def gathered_copies(array, axis, dim):
    parts = copy_for_each(array, axis)
    return laid_out(parts, dim)


def padded_to(lines, peers):
    spare = -len(lines) % peers
    return jnp.pad(lines, [(0, spare)] + [(0, 0)] * (lines.ndim - 1))


def sum_by_parts(array, axis):
    lines = array.reshape(-1, *array.shape[1:][-1:])
    own = lax.psum_scatter(
        padded_to(lines, lax.axis_size(axis)), axis, scatter_dimension=0, tiled=True
    )
    whole = lax.all_gather(own, axis).reshape(-1, *lines.shape[1:])
    return lax.slice_in_dim(whole, 0, len(lines)).reshape(array.shape)


def shifted(block, axis, distance):
    devices = range(lax.axis_size(axis))
    route = [(i - distance, i) for i in devices if i - distance in devices]
    return lax.ppermute(block, axis, route)


def orthonormal(summed):
    gram = jnp.einsum("kb,lb->kl", summed, summed, precision=lax.Precision.HIGHEST)
    chol = jnp.linalg.cholesky(gram)
    return jax.scipy.linalg.solve_triangular(chol, summed, lower=True).astype(jnp.bfloat16)


def local(panel, diag_tiles, dinv, u_fac, v_fac, ranks, sketch):
    left_factor = u_fac[0, :, 0]
    right_factor = v_fac[0, :, 0]
    slots = lax.broadcasted_iota(jnp.int32, (1, left_factor.shape[1], 1), 1)
    keep = slots < ranks[0, :, 0][:, None, None]
    random_probe = jnp.einsum(
        "jef,yf->jey", right_factor, sketch[0], preferred_element_type=jnp.float32
    )
    random_probe = jnp.where(keep, random_probe, 0.0).astype(jnp.bfloat16)
    range_component = jnp.einsum(
        "zgj,zgp->zpj", left_factor, random_probe, preferred_element_type=jnp.float32
    )
    share = sum_at_owner(range_component.astype(jnp.bfloat16), "upd", 0)
    range_basis = gathered_copies(jax.vmap(orthonormal)(share), "upd", 0)
    coefficient_matrix = jnp.einsum(
        "wxj,wuj->wxu", left_factor, range_basis, preferred_element_type=jnp.float32
    )
    coefficient_matrix = jnp.where(keep, coefficient_matrix, 0.0).astype(jnp.bfloat16)
    cross_term_part = jnp.einsum(
        "zgj,zgp->zpj", right_factor, coefficient_matrix, preferred_element_type=jnp.float32
    )
    cross_term = (
        sum_by_parts(cross_term_part.astype(jnp.bfloat16), "upd")
        .astype(jnp.float32)
        .astype(jnp.bfloat16)
    )
    rows_dev = panel.shape[2]
    first_row = lax.axis_index("upd") * rows_dev
    range_basis_rows = lax.dynamic_slice_in_dim(range_basis, first_row, rows_dev, 2)
    approximation = jnp.einsum(
        "fei,fej->fij", range_basis_rows, cross_term, preferred_element_type=jnp.float32
    )
    updated_tile = (panel[0].astype(jnp.float32) - approximation).astype(jnp.bfloat16)
    lowrank_factor = jnp.einsum(
        "vxn,en->vxe", updated_tile, dinv[0], preferred_element_type=jnp.float32
    ).astype(jnp.bfloat16)
    band = lowrank_factor.shape[0]
    received = jnp.stack(
        [shifted(lowrank_factor[offset - 1], "col", offset) for offset in range(1, band + 1)]
    )
    columns = lax.all_to_all(received, "upd", split_axis=2, concat_axis=1, tiled=True)
    total = sum_at_owner(
        (-jnp.einsum("mrc,mnc->rn", columns, columns, preferred_element_type=jnp.float32)).astype(
            jnp.bfloat16
        ),
        "upd",
        0,
    )
    diag_out = (diag_tiles[0].astype(jnp.float32) + total)[None]
    return (lowrank_factor[None], diag_out)


def solution(mesh):
    in_specs = (
        P("col", None, "upd", None),
        P("col", "upd", None),
        P("col", None, None),
        P("col", None, "upd", None, None),
        P("col", None, "upd", None, None),
        P("col", None, "upd"),
        P("col", None, None),
    )
    out_specs = (P("col", None, "upd", None), P("col", "upd", None))
    return jax.shard_map(local, mesh=mesh, in_specs=in_specs, out_specs=out_specs, check_vma=False)
```

profile of v0, /device:TPU:160, one launch (start us, length us, event | category | flops | bytes accessed | tf_op | source)
XLA Modules:
  0.0 297.2 jit_solution(5002424032824517877)
XLA Ops:
  7.2 0.9 iota_compare_fusion.2
  8.1 2.9 fusion.21
  11.0 20.1 %all_to_all.33 = bf16[8,1,64,1024]{3,2,1,0:T(8,128)(2,1)S(1)} all-to-all(bf16[8,1,64,1024]{3,2,1,0:T(8,128)(2,1)S(1)} %fusion.21), channel_id=1, replica_groups=mesh['upd'=8,'col'=32] {'upd'}, dimensions={0} | all-to-all | bytes 2097152 | tf_op jit(solution)/shard_map/all_to_all | solution.py:15
  31.7 5.8 %custom-call.8 = f32[1,64,64]{2,1,0:T(8,128)S(1)} custom-call(f32[1,64,64]{2,1,0:T(8,128)S(1)} %fusion.53), custom_call_target="Cholesky" | custom-call | tf_op jit(solution)/shard_map/vmap(jit(cholesky))/cholesky | solution.py:59
  38.9 4.9 %custom-call.9 = f32[1,1,64,64]{2,3,1,0:T(8,128)S(1)} custom-call(f32[1,1,64,64]{3,2,1,0:T(8,128)S(1)} %fusion.52), custom_call_target="InvertDiagBlocksLowerTriangular" | custom-call | tf_op jit(solution)/shard_map/vmap(jit(_solve_triangular))/triangular_solve | solution.py:60
  44.4 18.4 %all_to_all.34 = bf16[8,1,64,1024]{3,2,1,0:T(8,128)(2,1)S(1)} all-to-all(bf16[8,1,64,1024]{3,2,1,0:T(8,128)(2,1)S(1)} %broadcast_in_dim.36), channel_id=1, replica_groups=mesh['upd'=8,'col'=32] {'upd'}, dimensions={0} | all-to-all | bytes 2097152 | tf_op jit(solution)/shard_map/all_to_all | solution.py:21
  62.8 3.8 %fusion.15 = bf16[8,64,1024]{2,1,0:T(8,128)(2,1)} fusion(bf16[1,8,1,96,1024]{4,3,2,1,0:T(8,128)(2,1)} %param.11, bf16[1,8,1,96,1024]{4,3,2,1,0:T(8,128)(2,1)} %param.10, bf16[8,1,64,1024]{3,2,1,0:T(8,128)(2,1)S(1)} %all_to_all.34, pred[8,96]{1,0:T(8,128)(4,1)S(1)} %iota_compare_fusion.2), kind=kOutput, calls=%fused_computation.17 | convolution fusion | flops 201949184 | bytes 5243648 | tf_op jit(solution)/shard_map/zgj,zgp->zpj/dot_general | solution.py:81
  66.7 34.1 %reduce-scatter.2.cloned.1.call-done = bf16[64,1024]{1,0:T(8,128)(2,1)} async-done(((bf16[512,1024]{1,0:T(8,128)(2,1)}), bf16[64,1024]{1,0:T(8,128)(2,1)}) %reduce-scatter.2.cloned.1.call-update) | async-done | bytes 131088 | tf_op jit(solution)/shard_map/reduce_scatter | solution.py:44
  100.8 26.5 %all-gather.3.cloned.1.call-done = bf16[512,1024]{1,0:T(8,128)(2,1)} async-done(((bf16[64,1024]{1,0:T(8,128)(2,1)}), bf16[512,1024]{1,0:T(8,128)(2,1)}) %all-gather.3.cloned.1.call-update) | async-done | bytes 1048592 | tf_op jit(solution)/shard_map/all_gather | solution.py:47
  127.3 6.2 %fusion.4 = bf16[8,128,1024]{2,1,0:T(8,128)(2,1)} fusion(bf16[1,1024,1024]{2,1,0:T(8,128)(2,1)S(1)} %copy-done, bf16[8,64,1024]{2,1,0:T(8,128)(2,1)} %bitcast.126, bf16[1,8,128,1024]{3,2,1,0:T(8,128)(2,1)} %param.7, bf16[8,1,64,1024]{3,2,1,0:T(8,128)(2,1)S(1)} %all_to_all.34, s32[]{:T(128)S(6)} %select_n.17), kind=kOutput, calls=%fused_computation.8 | convolution fusion | flops 2285895680 | bytes 7471108 | tf_op jit(solution)/shard_map/vxn,en->vxe/dot_general | solution.py:96
  133.6 1.7 slice_bitcast_fusion
  135.3 3.4 %collective-permute-start = (bf16[128,1024]{1,0:T(8,128)(2,1)S(1)}, bf16[128,1024]{1,0:T(8,128)(2,1)S(1)}, u32[]{:S(2)}, u32[]{:S(2)}) collective-permute-start(bf16[128,1024]{1,0:T(8,128)(2,1)S(1)} %get-tuple-element.9), channel_id=1, source_target_pairs={{0,1},{1,2},{2,3},{3,4},{4,5},{5,6},{6,7},{7,8},{8,9},{9,10},{10,1... | collective-permute-start | bytes 786440 | tf_op jit(solution)/shard_map/ppermute | solution.py:54
  138.7 4.6 %collective-permute-start.1 = (bf16[128,1024]{1,0:T(8,128)(2,1)S(1)}, bf16[128,1024]{1,0:T(8,128)(2,1)S(1)}, u32[]{:S(2)}, u32[]{:S(2)}) collective-permute-start(bf16[128,1024]{1,0:T(8,128)(2,1)S(1)} %get-tuple-element.8), channel_id=1, source_target_pairs={{0,2},{1,3},{2,4},{3,5},{4,6},{5,7},{6,8},{7,9},{8,10},{9,11},{10,... | collective-permute-start | bytes 786440 | tf_op jit(solution)/shard_map/ppermute | solution.py:54
  143.3 2.7 collective-permute-start.7
  146.0 2.2 collective-permute-start.6
  148.2 1.9 collective-permute-start.5
  150.2 4.9 %collective-permute-start.2 = (bf16[128,1024]{1,0:T(8,128)(2,1)S(1)}, bf16[128,1024]{1,0:T(8,128)(2,1)S(1)}, u32[]{:S(2)}, u32[]{:S(2)}) collective-permute-start(bf16[128,1024]{1,0:T(8,128)(2,1)S(1)} %get-tuple-element.7), channel_id=1, source_target_pairs={{0,3},{1,4},{2,5},{3,6},{4,7},{5,8},{6,9},{7,10},{8,11},{9,12},{10... | collective-permute-start | bytes 786440 | tf_op jit(solution)/shard_map/ppermute | solution.py:54
  155.1 0.7 bitcast_dynamic-update-slice_fusion.7
  155.8 2.6 collective-permute-start.3
  159.1 22.9 %collective-permute-done.2 = bf16[128,1024]{1,0:T(8,128)(2,1)S(1)} collective-permute-done((bf16[128,1024]{1,0:T(8,128)(2,1)S(1)}, bf16[128,1024]{1,0:T(8,128)(2,1)S(1)}, u32[]{:S(2)}, u32[]{:S(2)}) %collective-permute-start.2) | collective-permute-done | bytes 262176 | tf_op jit(solution)/shard_map/ppermute | solution.py:54
  182.1 13.4 %collective-permute-start.4 = (bf16[128,1024]{1,0:T(8,128)(2,1)S(1)}, bf16[128,1024]{1,0:T(8,128)(2,1)S(1)}, u32[]{:S(2)}, u32[]{:S(2)}) collective-permute-start(bf16[128,1024]{1,0:T(8,128)(2,1)S(1)} %get-tuple-element.5), channel_id=1, source_target_pairs={{0,5},{1,6},{2,7},{3,8},{4,9},{5,10},{6,11},{7,12},{8,13},{9,14},{... | collective-permute-start | bytes 786440 | tf_op jit(solution)/shard_map/ppermute | solution.py:54
  195.5 0.7 bitcast_dynamic-update-slice_fusion.5
  196.2 0.7 bitcast_dynamic-update-slice_fusion.4
  197.0 14.6 %collective-permute-done.4 = bf16[128,1024]{1,0:T(8,128)(2,1)S(1)} collective-permute-done((bf16[128,1024]{1,0:T(8,128)(2,1)S(1)}, bf16[128,1024]{1,0:T(8,128)(2,1)S(1)}, u32[]{:S(2)}, u32[]{:S(2)}) %collective-permute-start.4) | collective-permute-done | bytes 262176 | tf_op jit(solution)/shard_map/ppermute | solution.py:54
  212.3 0.7 bitcast_dynamic-update-slice_fusion.2
  213.8 0.7 bitcast_dynamic-update-slice_fusion
  214.5 4.2 %copy.15 = bf16[8,128,1024]{1,0,2:T(8,128)(2,1)} copy(bf16[8,128,1024]{2,1,0:T(8,128)(2,1)} %bitcast_dynamic-update-slice_fusion) | data formatting | bytes 4194304 | tf_op jit(solution)/shard_map/stack | solution.py:100
  218.7 31.6 %all_to_all.35 = bf16[8,128,1024]{1,0,2:T(8,128)(2,1)} all-to-all(bf16[8,128,1024]{1,0,2:T(8,128)(2,1)} %copy.15), channel_id=1, replica_groups=mesh['upd'=8,'col'=32] {'upd'}, dimensions={2} | all-to-all | bytes 4194304 | tf_op jit(solution)/shard_map/all_to_all | solution.py:103
  250.2 4.1 %copy.16 = bf16[8,128,8,128]{3,1,2,0:T(8,128)(2,1)} copy(bf16[8,128,8,128]{1,0,3,2:T(8,128)(2,1)} %bitcast.120) | data formatting | bytes 4194304 | tf_op jit(solution)/shard_map/all_to_all | solution.py:103
  254.4 4.6 %fusion.1 = bf16[1024,1024]{1,0:T(8,128)(2,1)S(1)} fusion(bf16[8,1024,128]{2,1,0:T(8,128)(2,1)} %bitcast.123), kind=kOutput, calls=%fused_computation.3 | convolution fusion | flops 2149580800 | bytes 4194304 | tf_op jit(solution)/shard_map/mrc,mnc->rn/dot_general | solution.py:105
  258.9 29.7 %all_to_all.36 = bf16[8,128,1024]{2,1,0:T(8,128)(2,1)S(1)} all-to-all(bf16[8,128,1024]{2,1,0:T(8,128)(2,1)S(1)} %bitcast.124), channel_id=1, replica_groups=mesh['upd'=8,'col'=32] {'upd'}, dimensions={0} | all-to-all | bytes 4194304 | tf_op jit(solution)/shard_map/all_to_all | solution.py:15
  289.6 0.8 bitcast_add_fusion
  (27 shorter events, 5.8 us)
Async XLA Ops:
  7.2 120.2 %copy-start = (bf16[1,1024,1024]{2,1,0:T(8,128)(2,1)S(1)}, bf16[1,1024,1024]{2,1,0:T(8,128)(2,1)}, u32[]{:S(2)}) copy-start(bf16[1,1024,1024]{2,1,0:T(8,128)(2,1)} %param.9) | copy-start | bytes 6291460
  7.2 93.6 %reduce-scatter.2.cloned.1.call-start = ((), (), s32[]{:S(2)}) async-start(), calls=%async_computation.5 | async-start | bytes 1179648 | tf_op jit(solution)/shard_map/reduce_scatter | solution.py:44
  66.6 60.7 %all-gather.3.cloned.1.call-start = ((), (), s32[]{:S(2)}) async-start(), calls=%async_computation.6 | async-start | bytes 1179648 | tf_op jit(solution)/shard_map/all_gather | solution.py:47
  135.3 14.9 %collective-permute-start = (bf16[128,1024]{1,0:T(8,128)(2,1)S(1)}, bf16[128,1024]{1,0:T(8,128)(2,1)S(1)}, u32[]{:S(2)}, u32[]{:S(2)}) collective-permute-start(bf16[128,1024]{1,0:T(8,128)(2,1)S(1)} %get-tuple-element.9), channel_id=1, source_target_pairs={{0,1},{1,2},{2,3},{3,4},{4,5},{5,6},{6,7},{7,8},{8,9},{9,10},{10,1... | collective-permute-start | bytes 786440 | tf_op jit(solution)/shard_map/ppermute | solution.py:54
  138.7 17.1 %collective-permute-start.1 = (bf16[128,1024]{1,0:T(8,128)(2,1)S(1)}, bf16[128,1024]{1,0:T(8,128)(2,1)S(1)}, u32[]{:S(2)}, u32[]{:S(2)}) collective-permute-start(bf16[128,1024]{1,0:T(8,128)(2,1)S(1)} %get-tuple-element.8), channel_id=1, source_target_pairs={{0,2},{1,3},{2,4},{3,5},{4,6},{5,7},{6,8},{7,9},{8,10},{9,11},{10,... | collective-permute-start | bytes 786440 | tf_op jit(solution)/shard_map/ppermute | solution.py:54
  143.3 70.4 %collective-permute-start.7 = (bf16[128,1024]{1,0:T(8,128)(2,1)S(1)}, bf16[128,1024]{1,0:T(8,128)(2,1)S(1)}, u32[]{:S(2)}, u32[]{:S(2)}) collective-permute-start(bf16[128,1024]{1,0:T(8,128)(2,1)S(1)} %get-tuple-element.2), channel_id=1, source_target_pairs={{0,8},{1,9},{2,10},{3,11},{4,12},{5,13},{6,14},{7,15},{8,16},{9,17... | collective-permute-start | bytes 786440 | tf_op jit(solution)/shard_map/ppermute | solution.py:54
  146.0 67.1 %collective-permute-start.6 = (bf16[128,1024]{1,0:T(8,128)(2,1)S(1)}, bf16[128,1024]{1,0:T(8,128)(2,1)S(1)}, u32[]{:S(2)}, u32[]{:S(2)}) collective-permute-start(bf16[128,1024]{1,0:T(8,128)(2,1)S(1)} %get-tuple-element.3), channel_id=1, source_target_pairs={{0,7},{1,8},{2,9},{3,10},{4,11},{5,12},{6,13},{7,14},{8,15},{9,16}... | collective-permute-start | bytes 786440 | tf_op jit(solution)/shard_map/ppermute | solution.py:54
  148.2 64.1 %collective-permute-start.5 = (bf16[128,1024]{1,0:T(8,128)(2,1)S(1)}, bf16[128,1024]{1,0:T(8,128)(2,1)S(1)}, u32[]{:S(2)}, u32[]{:S(2)}) collective-permute-start(bf16[128,1024]{1,0:T(8,128)(2,1)S(1)} %get-tuple-element.4), channel_id=1, source_target_pairs={{0,6},{1,7},{2,8},{3,9},{4,10},{5,11},{6,12},{7,13},{8,14},{9,15},... | collective-permute-start | bytes 786440 | tf_op jit(solution)/shard_map/ppermute | solution.py:54
  150.2 31.8 %collective-permute-start.2 = (bf16[128,1024]{1,0:T(8,128)(2,1)S(1)}, bf16[128,1024]{1,0:T(8,128)(2,1)S(1)}, u32[]{:S(2)}, u32[]{:S(2)}) collective-permute-start(bf16[128,1024]{1,0:T(8,128)(2,1)S(1)} %get-tuple-element.7), channel_id=1, source_target_pairs={{0,3},{1,4},{2,5},{3,6},{4,7},{5,8},{6,9},{7,10},{8,11},{9,12},{10... | collective-permute-start | bytes 786440 | tf_op jit(solution)/shard_map/ppermute | solution.py:54
  155.8 40.4 %collective-permute-start.3 = (bf16[128,1024]{1,0:T(8,128)(2,1)S(1)}, bf16[128,1024]{1,0:T(8,128)(2,1)S(1)}, u32[]{:S(2)}, u32[]{:S(2)}) collective-permute-start(bf16[128,1024]{1,0:T(8,128)(2,1)S(1)} %get-tuple-element.6), channel_id=1, source_target_pairs={{0,4},{1,5},{2,6},{3,7},{4,8},{5,9},{6,10},{7,11},{8,12},{9,13},{1... | collective-permute-start | bytes 786440 | tf_op jit(solution)/shard_map/ppermute | solution.py:54
  182.1 29.5 %collective-permute-start.4 = (bf16[128,1024]{1,0:T(8,128)(2,1)S(1)}, bf16[128,1024]{1,0:T(8,128)(2,1)S(1)}, u32[]{:S(2)}, u32[]{:S(2)}) collective-permute-start(bf16[128,1024]{1,0:T(8,128)(2,1)S(1)} %get-tuple-element.5), channel_id=1, source_target_pairs={{0,5},{1,6},{2,7},{3,8},{4,9},{5,10},{6,11},{7,12},{8,13},{9,14},{... | collective-permute-start | bytes 786440 | tf_op jit(solution)/shard_map/ppermute | solution.py:54
  288.6 1.0 copy-start.1
Sparse Core Ops, SparseCore 0:
  66.8 33.9 reduce-scatter.1
  102.7 24.6 all-gather.2
where the time goes:
time: 298 us; the launch traced here: 297 us
  blocking collectives  99.7 us (33%)
  waiting for transfers between devices  98.3 us (33%)
  starting transfers between devices  35.7 us (12%)
  matrix products  18.4 us (6%)
  local copies, waits for them, and re-layouts  16.6 us (6%)
  other arithmetic  14.3 us (5%)
  between operations  14.2 us (5%)
    all_to_all x2, blocking collectives, sum_at_owner(): lax.all_to_all(parts, axis, split_axis=0, concat_axis=0, tiled=True)  49.7 us
    ppermute x8, waiting for transfers between devices, shifted(): return lax.ppermute(block, axis, route)  37.7 us
    ppermute x8, starting transfers between devices, shifted(): return lax.ppermute(block, axis, route)  35.6 us
    reduce_scatter x1, waiting for transfers between devices, sum_by_parts(): lax.psum_scatter(padded_to(lines, lax.axis_size(axis)), axis, scatter_dim...  34.1 us
    all_to_all x1, blocking collectives, local(): lax.all_to_all(received, 'upd', split_axis=2, concat_axis=1, tiled=True)  31.6 us
    all_gather x1, waiting for transfers between devices, sum_by_parts(): whole = lax.all_gather(own, axis).reshape(-1, *lines.shape[1:])  26.5 us
    all_to_all x1, blocking collectives, copy_for_each(): lax.all_to_all(jnp.broadcast_to(array[None], (peers, *array.shape)), axis...  18.4 us
    another operation x3, other arithmetic, orthonormal(): chol = jnp.linalg.cholesky(gram)  6.52 us
  transfers between devices with their start and end apart: 10, of which 5 were waited for; matrix products, arithmetic and copies ran while one was open for 2% of the time, Pallas kernels for 0%

commit v1 on v0

--- a/solution.py
+++ b/solution.py
@@ -100,7 +100,10 @@
     received = jnp.stack(
         [shifted(lowrank_factor[offset - 1], "col", offset) for offset in range(1, band + 1)]
     )
-    columns = lax.all_to_all(received, "upd", split_axis=2, concat_axis=1, tiled=True)
+    columns = jnp.concatenate(
+        lax.all_to_all(jnp.stack(jnp.split(received, lax.axis_size("upd"), axis=2)), "upd", 0, 0),
+        axis=1,
+    )
     total = sum_at_owner(
         (-jnp.einsum("mrc,mnc->rn", columns, columns, preferred_element_type=jnp.float32)).astype(
             jnp.bfloat16

time: 298 us -> 284 us (0.953)
  local copies, waits for them, and re-layouts: 16.6 us -> 3.61 us
    another operation x2 -> x1, local copies, waits for them, and re-layouts: 4.88 us -> 0.02 us  [local(): jnp.stack([shifted(lowrank_factor[offset - 1], 'col', offset) for offset...]
    unnamed x11 -> x18, local copies, waits for them, and re-layouts: 5.71 us -> 1.34 us
    all_to_all x1 -> x0, local copies, waits for them, and re-layouts: 4.13 us -> none  [local(): lax.all_to_all(received, 'upd', split_axis=2, concat_axis=1, tiled=True)]
  transfers between devices with their start and end apart: 10 -> 10, of which waited for: 5 -> 5; matrix products, arithmetic and copies ran while one was open for 2% -> 0% of each run, Pallas kernels for 0% -> 0%
where the time goes in v1:
time: 284 us; the launch traced here: 283 us
  waiting for transfers between devices  101 us (36%)
  blocking collectives  98 us (35%)
  starting transfers between devices  35.7 us (13%)
  matrix products  16.2 us (6%)
  between operations  14.4 us (5%)
  other arithmetic  14.3 us (5%)
  local copies, waits for them, and re-layouts  3.61 us (1%)
    all_to_all x2, blocking collectives, sum_at_owner(): lax.all_to_all(parts, axis, split_axis=0, concat_axis=0, tiled=True)  49.7 us
    ppermute x8, waiting for transfers between devices, shifted(): return lax.ppermute(block, axis, route)  40.5 us
    ppermute x8, starting transfers between devices, shifted(): return lax.ppermute(block, axis, route)  35.7 us
    reduce_scatter x1, waiting for transfers between devices, sum_by_parts(): lax.psum_scatter(padded_to(lines, lax.axis_size(axis)), axis, scatter_dim...  34.1 us
    all_to_all x1, blocking collectives, local(): lax.all_to_all(jnp.stack(jnp.split(received, lax.axis_size('upd'), axis=2...  29.9 us
    all_gather x1, waiting for transfers between devices, sum_by_parts(): whole = lax.all_gather(own, axis).reshape(-1, *lines.shape[1:])  26.5 us
    all_to_all x1, blocking collectives, copy_for_each(): lax.all_to_all(jnp.broadcast_to(array[None], (peers, *array.shape)), axis...  18.4 us
    another operation x3, other arithmetic, orthonormal(): chol = jnp.linalg.cholesky(gram)  6.52 us
  transfers between devices with their start and end apart: 10, of which 5 were waited for; matrix products, arithmetic and copies ran while one was open for 0% of the time, Pallas kernels for 0%

profile of v1, /device:TPU:160, one launch (start us, length us, event | category | flops | bytes accessed | tf_op | source)
XLA Modules:
  0.0 283.3 jit_solution(11677934313091907578)
XLA Ops:
  7.2 0.9 iota_compare_fusion.2
  8.1 2.9 %fusion.21 = bf16[8,1,64,1024]{3,2,1,0:T(8,128)(2,1)S(1)} fusion(bf16[1,8,1,96,1024]{4,3,2,1,0:T(8,128)(2,1)} %param.10, bf16[1,8,1,96,1024]{4,3,2,1,0:T(8,128)(2,1)} %param.11, bf16[1,64,1024]{2,1,0:T(8,128)(2,1)} %param.13, pred[8,96]{1,0:T(8,128)(4,1)S(1)} %iota_compare_fusion.2), kind=kOutput, calls=%fused_computation.19 | convolution fusion | flops 201949184 | bytes 4326144 | tf_op jit(solution)/shard_map/zgj,zgp->zpj/dot_general | solution.py:72
  11.0 20.1 %all_to_all.20 = bf16[8,1,64,1024]{3,2,1,0:T(8,128)(2,1)S(1)} all-to-all(bf16[8,1,64,1024]{3,2,1,0:T(8,128)(2,1)S(1)} %fusion.21), channel_id=1, replica_groups=mesh['upd'=8,'col'=32] {'upd'}, dimensions={0} | all-to-all | bytes 2097152 | tf_op jit(solution)/shard_map/all_to_all | solution.py:15
  31.3 0.4 fusion.67
  31.7 5.8 %custom-call.8 = f32[1,64,64]{2,1,0:T(8,128)S(1)} custom-call(f32[1,64,64]{2,1,0:T(8,128)S(1)} %fusion.61), custom_call_target="Cholesky" | custom-call | tf_op jit(solution)/shard_map/vmap(jit(cholesky))/cholesky | solution.py:59
  37.6 0.6 compare_reduce_fusion
  38.3 0.7 fusion.60
  38.9 4.9 %custom-call.9 = f32[1,1,64,64]{2,3,1,0:T(8,128)S(1)} custom-call(f32[1,1,64,64]{3,2,1,0:T(8,128)S(1)} %fusion.60), custom_call_target="InvertDiagBlocksLowerTriangular" | custom-call | tf_op jit(solution)/shard_map/vmap(jit(_solve_triangular))/triangular_solve | solution.py:60
  43.8 0.4 convolution_convert_fusion
  44.4 18.4 %all_to_all.21 = bf16[8,1,64,1024]{3,2,1,0:T(8,128)(2,1)S(1)} all-to-all(bf16[8,1,64,1024]{3,2,1,0:T(8,128)(2,1)S(1)} %broadcast_in_dim.36), channel_id=1, replica_groups=mesh['upd'=8,'col'=32] {'upd'}, dimensions={0} | all-to-all | bytes 2097152 | tf_op jit(solution)/shard_map/all_to_all | solution.py:21
  62.8 3.8 %fusion.15 = bf16[8,64,1024]{2,1,0:T(8,128)(2,1)} fusion(bf16[1,8,1,96,1024]{4,3,2,1,0:T(8,128)(2,1)} %param.11, bf16[1,8,1,96,1024]{4,3,2,1,0:T(8,128)(2,1)} %param.10, bf16[8,1,64,1024]{3,2,1,0:T(8,128)(2,1)S(1)} %all_to_all.21, pred[8,96]{1,0:T(8,128)(4,1)S(1)} %iota_compare_fusion.2), kind=kOutput, calls=%fused_computation.17 | convolution fusion | flops 201949184 | bytes 5243648 | tf_op jit(solution)/shard_map/zgj,zgp->zpj/dot_general | solution.py:81
  66.7 34.1 %reduce-scatter.2.cloned.1.call-done = bf16[64,1024]{1,0:T(8,128)(2,1)} async-done(((bf16[512,1024]{1,0:T(8,128)(2,1)}), bf16[64,1024]{1,0:T(8,128)(2,1)}) %reduce-scatter.2.cloned.1.call-update) | async-done | bytes 131088 | tf_op jit(solution)/shard_map/reduce_scatter | solution.py:44
  100.8 26.5 %all-gather.3.cloned.1.call-done = bf16[512,1024]{1,0:T(8,128)(2,1)} async-done(((bf16[64,1024]{1,0:T(8,128)(2,1)}), bf16[512,1024]{1,0:T(8,128)(2,1)}) %all-gather.3.cloned.1.call-update) | async-done | bytes 1048592 | tf_op jit(solution)/shard_map/all_gather | solution.py:47
  127.3 6.2 %fusion.4 = bf16[8,128,1024]{2,1,0:T(8,128)(2,1)} fusion(bf16[1,1024,1024]{2,1,0:T(8,128)(2,1)S(1)} %copy-done, bf16[8,64,1024]{2,1,0:T(8,128)(2,1)} %bitcast.156, bf16[1,8,128,1024]{3,2,1,0:T(8,128)(2,1)} %param.7, bf16[8,1,64,1024]{3,2,1,0:T(8,128)(2,1)S(1)} %all_to_all.21, s32[]{:T(128)S(6)} %select_n.17), kind=kOutput, calls=%fused_computation.8 | convolution fusion | flops 2285895680 | bytes 7471108 | tf_op jit(solution)/shard_map/vxn,en->vxe/dot_general | solution.py:96
  133.6 1.7 slice_bitcast_fusion.8
  135.3 3.4 %collective-permute-start = (bf16[128,1024]{1,0:T(8,128)(2,1)S(1)}, bf16[128,1024]{1,0:T(8,128)(2,1)S(1)}, u32[]{:S(2)}, u32[]{:S(2)}) collective-permute-start(bf16[128,1024]{1,0:T(8,128)(2,1)S(1)} %get-tuple-element.9), channel_id=1, source_target_pairs={{0,1},{1,2},{2,3},{3,4},{4,5},{5,6},{6,7},{7,8},{8,9},{9,10},{10,1... | collective-permute-start | bytes 786440 | tf_op jit(solution)/shard_map/ppermute | solution.py:54
  138.7 4.6 %collective-permute-start.1 = (bf16[128,1024]{1,0:T(8,128)(2,1)S(1)}, bf16[128,1024]{1,0:T(8,128)(2,1)S(1)}, u32[]{:S(2)}, u32[]{:S(2)}) collective-permute-start(bf16[128,1024]{1,0:T(8,128)(2,1)S(1)} %get-tuple-element.8), channel_id=1, source_target_pairs={{0,2},{1,3},{2,4},{3,5},{4,6},{5,7},{6,8},{7,9},{8,10},{9,11},{10,... | collective-permute-start | bytes 786440 | tf_op jit(solution)/shard_map/ppermute | solution.py:54
  143.3 2.7 collective-permute-start.7
  146.0 2.2 collective-permute-start.6
  148.2 1.9 collective-permute-start.5
  150.2 4.9 %collective-permute-start.2 = (bf16[128,1024]{1,0:T(8,128)(2,1)S(1)}, bf16[128,1024]{1,0:T(8,128)(2,1)S(1)}, u32[]{:S(2)}, u32[]{:S(2)}) collective-permute-start(bf16[128,1024]{1,0:T(8,128)(2,1)S(1)} %get-tuple-element.7), channel_id=1, source_target_pairs={{0,3},{1,4},{2,5},{3,6},{4,7},{5,8},{6,9},{7,10},{8,11},{9,12},{10... | collective-permute-start | bytes 786440 | tf_op jit(solution)/shard_map/ppermute | solution.py:54
  155.1 2.6 collective-permute-start.3
  157.7 24.3 %collective-permute-done.2 = bf16[128,1024]{1,0:T(8,128)(2,1)S(1)} collective-permute-done((bf16[128,1024]{1,0:T(8,128)(2,1)S(1)}, bf16[128,1024]{1,0:T(8,128)(2,1)S(1)}, u32[]{:S(2)}, u32[]{:S(2)}) %collective-permute-start.2) | collective-permute-done | bytes 262176 | tf_op jit(solution)/shard_map/ppermute | solution.py:54
  182.1 13.4 %collective-permute-start.4 = (bf16[128,1024]{1,0:T(8,128)(2,1)S(1)}, bf16[128,1024]{1,0:T(8,128)(2,1)S(1)}, u32[]{:S(2)}, u32[]{:S(2)}) collective-permute-start(bf16[128,1024]{1,0:T(8,128)(2,1)S(1)} %get-tuple-element.5), channel_id=1, source_target_pairs={{0,5},{1,6},{2,7},{3,8},{4,9},{5,10},{6,11},{7,12},{8,13},{9,14},{... | collective-permute-start | bytes 786440 | tf_op jit(solution)/shard_map/ppermute | solution.py:54
  195.6 16.0 %collective-permute-done.4 = bf16[128,1024]{1,0:T(8,128)(2,1)S(1)} collective-permute-done((bf16[128,1024]{1,0:T(8,128)(2,1)S(1)}, bf16[128,1024]{1,0:T(8,128)(2,1)S(1)}, u32[]{:S(2)}, u32[]{:S(2)}) %collective-permute-start.4) | collective-permute-done | bytes 262176 | tf_op jit(solution)/shard_map/ppermute | solution.py:54
  212.5 29.9 %all_to_all.22 = bf16[8,8,128,128]{3,2,1,0:T(8,128)(2,1)S(1)} all-to-all(bf16[8,8,128,128]{3,2,1,0:T(8,128)(2,1)S(1)} %fusion.42), channel_id=1, replica_groups=mesh['upd'=8,'col'=32] {'upd'}, dimensions={0} | all-to-all | bytes 4194304 | tf_op jit(solution)/shard_map/all_to_all | solution.py:104
  242.4 0.2 copy.21
  242.6 2.4 fusion.1
  245.0 29.7 %all_to_all.23 = bf16[8,128,1024]{2,1,0:T(8,128)(2,1)S(1)} all-to-all(bf16[8,128,1024]{2,1,0:T(8,128)(2,1)S(1)} %bitcast.154), channel_id=1, replica_groups=mesh['upd'=8,'col'=32] {'upd'}, dimensions={0} | all-to-all | bytes 4194304 | tf_op jit(solution)/shard_map/all_to_all | solution.py:15
  274.6 0.4 convert_reduce_fusion
  275.0 0.6 copy-done.1
  275.6 0.8 bitcast_add_fusion
  (34 shorter events, 1.5 us)
Async XLA Ops:
  7.2 120.2 %copy-start = (bf16[1,1024,1024]{2,1,0:T(8,128)(2,1)S(1)}, bf16[1,1024,1024]{2,1,0:T(8,128)(2,1)}, u32[]{:S(2)}) copy-start(bf16[1,1024,1024]{2,1,0:T(8,128)(2,1)} %param.9) | copy-start | bytes 6291460
  7.2 93.6 %reduce-scatter.2.cloned.1.call-start = ((), (), s32[]{:S(2)}) async-start(), calls=%async_computation.5 | async-start | bytes 1179648 | tf_op jit(solution)/shard_map/reduce_scatter | solution.py:44
  66.6 60.7 %all-gather.3.cloned.1.call-start = ((), (), s32[]{:S(2)}) async-start(), calls=%async_computation.6 | async-start | bytes 1179648 | tf_op jit(solution)/shard_map/all_gather | solution.py:47
  135.3 14.9 %collective-permute-start = (bf16[128,1024]{1,0:T(8,128)(2,1)S(1)}, bf16[128,1024]{1,0:T(8,128)(2,1)S(1)}, u32[]{:S(2)}, u32[]{:S(2)}) collective-permute-start(bf16[128,1024]{1,0:T(8,128)(2,1)S(1)} %get-tuple-element.9), channel_id=1, source_target_pairs={{0,1},{1,2},{2,3},{3,4},{4,5},{5,6},{6,7},{7,8},{8,9},{9,10},{10,1... | collective-permute-start | bytes 786440 | tf_op jit(solution)/shard_map/ppermute | solution.py:54
  138.7 16.4 %collective-permute-start.1 = (bf16[128,1024]{1,0:T(8,128)(2,1)S(1)}, bf16[128,1024]{1,0:T(8,128)(2,1)S(1)}, u32[]{:S(2)}, u32[]{:S(2)}) collective-permute-start(bf16[128,1024]{1,0:T(8,128)(2,1)S(1)} %get-tuple-element.8), channel_id=1, source_target_pairs={{0,2},{1,3},{2,4},{3,5},{4,6},{5,7},{6,8},{7,9},{8,10},{9,11},{10,... | collective-permute-start | bytes 786440 | tf_op jit(solution)/shard_map/ppermute | solution.py:54
  143.3 68.4 %collective-permute-start.7 = (bf16[128,1024]{1,0:T(8,128)(2,1)S(1)}, bf16[128,1024]{1,0:T(8,128)(2,1)S(1)}, u32[]{:S(2)}, u32[]{:S(2)}) collective-permute-start(bf16[128,1024]{1,0:T(8,128)(2,1)S(1)} %get-tuple-element.2), channel_id=1, source_target_pairs={{0,8},{1,9},{2,10},{3,11},{4,12},{5,13},{6,14},{7,15},{8,16},{9,17... | collective-permute-start | bytes 786440 | tf_op jit(solution)/shard_map/ppermute | solution.py:54
  146.0 65.7 %collective-permute-start.6 = (bf16[128,1024]{1,0:T(8,128)(2,1)S(1)}, bf16[128,1024]{1,0:T(8,128)(2,1)S(1)}, u32[]{:S(2)}, u32[]{:S(2)}) collective-permute-start(bf16[128,1024]{1,0:T(8,128)(2,1)S(1)} %get-tuple-element.3), channel_id=1, source_target_pairs={{0,7},{1,8},{2,9},{3,10},{4,11},{5,12},{6,13},{7,14},{8,15},{9,16}... | collective-permute-start | bytes 786440 | tf_op jit(solution)/shard_map/ppermute | solution.py:54
  148.2 63.4 %collective-permute-start.5 = (bf16[128,1024]{1,0:T(8,128)(2,1)S(1)}, bf16[128,1024]{1,0:T(8,128)(2,1)S(1)}, u32[]{:S(2)}, u32[]{:S(2)}) collective-permute-start(bf16[128,1024]{1,0:T(8,128)(2,1)S(1)} %get-tuple-element.4), channel_id=1, source_target_pairs={{0,6},{1,7},{2,8},{3,9},{4,10},{5,11},{6,12},{7,13},{8,14},{9,15},... | collective-permute-start | bytes 786440 | tf_op jit(solution)/shard_map/ppermute | solution.py:54
  150.2 31.8 %collective-permute-start.2 = (bf16[128,1024]{1,0:T(8,128)(2,1)S(1)}, bf16[128,1024]{1,0:T(8,128)(2,1)S(1)}, u32[]{:S(2)}, u32[]{:S(2)}) collective-permute-start(bf16[128,1024]{1,0:T(8,128)(2,1)S(1)} %get-tuple-element.7), channel_id=1, source_target_pairs={{0,3},{1,4},{2,5},{3,6},{4,7},{5,8},{6,9},{7,10},{8,11},{9,12},{10... | collective-permute-start | bytes 786440 | tf_op jit(solution)/shard_map/ppermute | solution.py:54
  155.1 40.4 %collective-permute-start.3 = (bf16[128,1024]{1,0:T(8,128)(2,1)S(1)}, bf16[128,1024]{1,0:T(8,128)(2,1)S(1)}, u32[]{:S(2)}, u32[]{:S(2)}) collective-permute-start(bf16[128,1024]{1,0:T(8,128)(2,1)S(1)} %get-tuple-element.6), channel_id=1, source_target_pairs={{0,4},{1,5},{2,6},{3,7},{4,8},{5,9},{6,10},{7,11},{8,12},{9,13},{1... | collective-permute-start | bytes 786440 | tf_op jit(solution)/shard_map/ppermute | solution.py:54
  182.1 29.5 %collective-permute-start.4 = (bf16[128,1024]{1,0:T(8,128)(2,1)S(1)}, bf16[128,1024]{1,0:T(8,128)(2,1)S(1)}, u32[]{:S(2)}, u32[]{:S(2)}) collective-permute-start(bf16[128,1024]{1,0:T(8,128)(2,1)S(1)} %get-tuple-element.5), channel_id=1, source_target_pairs={{0,5},{1,6},{2,7},{3,8},{4,9},{5,10},{6,11},{7,12},{8,13},{9,14},{... | collective-permute-start | bytes 786440 | tf_op jit(solution)/shard_map/ppermute | solution.py:54
  274.6 1.0 copy-start.1
Sparse Core Ops, SparseCore 0:
  66.8 33.9 reduce-scatter.1
  102.7 24.6 all-gather.2
